TPU v7x, 32 devices: a whole 2x2x4 slice. The times are simulated.
32 devices in a mesh: rep: 8 (over z, y), shard: 4 (over x, core).
Axes of the slice: x: 2, y: 2, z: 4, core: 2. Of those that a mesh axis runs over, the one named last changes fastest.
Arguments:
- tokens: bfloat16 [8, 1024, 2304], P('rep', 'shard'), may hold values from -6 to 6
- cotangent: bfloat16 [8, 1024, 2304], P('rep', 'shard'), may hold values from -6 to 6
- sequence_adapter_index: int32 [8], P('rep'), may hold values from 0 to 7
- image_span_start: int32 [8, 2], P('rep'), may hold values from 0 to 768, as said below
- attention_norm_gain: bfloat16 [2304], replicated, may hold values from 0.099609375 to 1.8984375
- feedforward_norm_gain: bfloat16 [2304], replicated, may hold values from 0.099609375 to 1.8984375
- query_key_value_weight: bfloat16 [3, 2304, 2304], P(None, 'shard'), may hold values from -0.125 to 0.125
- attention_output_weight: bfloat16 [2304, 2304], P('shard'), may hold values from -2 to 2
- gate_up_projection_weight: bfloat16 [2, 2304, 5760], P(None, 'shard'), may hold values from -0.125 to 0.125
- down_projection_weight: bfloat16 [5760, 2304], P('shard'), may hold values from -0.625 to 0.625
- adapter_model_input_maps: bfloat16 [6, 8, 16, 2304], P(None, 'shard'), may hold values from -0.125 to 0.125
- adapter_model_output_maps: bfloat16 [5, 8, 16, 2304], P(None, 'shard'), may hold values from -1.5 to 1.5
- adapter_hidden_input_map: bfloat16 [8, 16, 5760], P('shard'), may hold values from -0.078125 to 0.078125
- adapter_hidden_output_maps: bfloat16 [2, 8, 16, 5760], P(None, 'shard'), may hold values from -1.5 to 1.5
Outputs:
- output: bfloat16 [8, 1024, 2304], P('rep', 'shard')
- input_grad: float32 [8, 1024, 2304], P('rep', 'shard')
- grad_a_model: float32 [6, 8, 16, 2304], P(None, 'shard')
- grad_b_model: float32 [5, 8, 16, 2304], P(None, 'shard')
- grad_a_hidden: float32 [8, 16, 5760], P('shard')
- grad_b_hidden: float32 [2, 8, 16, 5760], P(None, 'shard')
Inputs may be any that keep to these rules, and one draw needn't show every extreme that they name: `image_span_start`: in each sequence the first span starts in 0 to 256 and the second in 512 to 768; some sequence's first span starts at 0 and some sequence's second span ends at the sequence's end.
All inputs are finite; a program needn't handle non-finite values.
Results may differ from a plain program's by a relative error of at most 0.023.
Values may be sent and summed in bfloat16 or wider, within the bound.
No kernel may reach another device: no remote copies, remote signals or barrier semaphores. Data moves between devices by JAX's collectives and lax.ppermute only.
A program may use at most 512 MiB of HBM per device.

v0:
```python
import math
import jax
import jax.numpy as jnp
from jax import lax
from jax.sharding import PartitionSpec as P

HDIM = 64
SPAN = 256
EPS = 1e-05
THETA = 10000.0
BRANCH = 1.4 / math.sqrt(40.0)


def norm_rows(values, gain):
    return values * lax.rsqrt(jnp.mean(values * values, axis=-1, keepdims=True) + EPS) * gain


def rotate(values, positions):
    rows = values.shape[0]
    heads = values.shape[1] // HDIM
    half = HDIM // 2
    exponent = jnp.arange(half, dtype=jnp.float32) * (-2.0 / HDIM)
    frequency = jnp.exp(exponent * math.log(THETA))
    angle = positions.astype(jnp.float32)[:, None] * frequency[None, :]
    cosine = jnp.concatenate([jnp.cos(angle), jnp.cos(angle)], axis=1)[:, None, :]
    sine = jnp.concatenate([jnp.sin(angle), jnp.sin(angle)], axis=1)[:, None, :]
    split = values.reshape(rows, heads, HDIM)
    turned = jnp.concatenate([-split[..., half:], split[..., :half]], axis=-1)
    return (split * cosine + turned * sine).reshape(rows, heads * HDIM)


def span_label(positions, starts):
    label = jnp.full(positions.shape, -1, jnp.int32)
    for number in range(starts.shape[0]):
        inside = (positions >= starts[number]) & (positions < starts[number] + SPAN)
        label = jnp.where(inside, jnp.int32(number), label)
    return label


def visible_pairs(rows, columns, starts):
    row_label = span_label(rows, starts)[:, None]
    column_label = span_label(columns, starts)[None, :]
    causal = columns[None, :] <= rows[:, None]
    return causal | (row_label == column_label) & (row_label >= 0)


def rounded_amount(values):
    return lax.optimization_barrier(values.astype(jnp.bfloat16)).astype(jnp.float32)


def heads_of(values):
    return values.reshape(values.shape[0], values.shape[1] // HDIM, HDIM)


def attention_scores(queries, keys, visible):
    raw = jnp.einsum(
        "qhd,khd->hqk", heads_of(queries), heads_of(keys), preferred_element_type=jnp.float32
    )
    return jnp.where(visible[None], raw * (1.0 / math.sqrt(HDIM)), -1e30)


def shards(
    tokens,
    cotangent,
    sequence_adapter_index,
    image_span_start,
    attention_norm_gain,
    feedforward_norm_gain,
    query_key_value_weight,
    attention_output_weight,
    gate_up_projection_weight,
    down_projection_weight,
    adapter_model_input_maps,
    adapter_model_output_maps,
    adapter_hidden_input_map,
    adapter_hidden_output_maps,
):
    local_rows = tokens.shape[1]
    width = tokens.shape[2]
    group = lax.axis_size("shard")
    place = lax.axis_index("shard")
    pick = sequence_adapter_index[0]
    starts = image_span_start[0]
    positions_local = place * local_rows + jnp.arange(local_rows, dtype=jnp.int32)
    positions_all = jnp.arange(local_rows * group, dtype=jnp.int32)
    visible = visible_pairs(positions_local, positions_all, starts)
    residual_in = tokens[0].astype(jnp.float32)
    gain_one = attention_norm_gain.astype(jnp.float32)
    gain_two = feedforward_norm_gain.astype(jnp.float32)
    a_model_all, b_model_all, a_hidden_all, b_hidden_all = (
        lax.all_gather(adapter_model_input_maps, "shard", axis=1, tiled=True),
        lax.all_gather(adapter_model_output_maps, "shard", axis=1, tiled=True),
        lax.all_gather(adapter_hidden_input_map[None], "shard", axis=1, tiled=True),
        lax.all_gather(adapter_hidden_output_maps, "shard", axis=1, tiled=True),
    )
    a_one = lax.dynamic_index_in_dim(a_model_all, pick, 1, keepdims=False)
    b_one = lax.dynamic_index_in_dim(b_model_all, pick, 1, keepdims=False)
    single_hidden_input_map = lax.dynamic_index_in_dim(a_hidden_all, pick, 1, keepdims=False)[0]
    b_hidden_one = lax.dynamic_index_in_dim(b_hidden_all, pick, 1, keepdims=False)
    normed = norm_rows(residual_in, gain_one).astype(jnp.bfloat16)
    empty = jnp.zeros((local_rows, width), jnp.float32)
    pieces = lax.all_gather(query_key_value_weight, "shard", axis=1, tiled=True)
    columns = normed
    base_query, base_key, base_value = tuple(
        (jnp.dot(columns, pieces[slot], preferred_element_type=jnp.float32) for slot in range(3))
    )
    narrow_first = jnp.einsum(
        "td,srd->str", normed, a_one[0:3], preferred_element_type=jnp.float32
    ).astype(jnp.bfloat16)
    lifted_first = jnp.einsum(
        "str,srd->std", narrow_first, b_one[0:3], preferred_element_type=jnp.float32
    )
    query = base_query + lifted_first[0]
    key_pre = base_key + lifted_first[1]
    value_low = (base_value + lifted_first[2]).astype(jnp.bfloat16)
    query_turned = rotate(query, positions_local).astype(jnp.bfloat16)
    key_turned = rotate(key_pre, positions_local).astype(jnp.bfloat16)
    keys_all, values_all = (
        lax.all_gather(key_turned, "shard", axis=0, tiled=True),
        lax.all_gather(value_low, "shard", axis=0, tiled=True),
    )
    scores = attention_scores(query_turned, keys_all, visible)
    top = jnp.max(scores, axis=-1, keepdims=True)
    weights = jnp.exp(scores - top)
    total = jnp.sum(weights, axis=-1, keepdims=True)
    log_total = top + jnp.log(total)
    probs = weights / total
    mixed = jnp.einsum(
        "hqk,khd->qhd",
        probs.astype(jnp.bfloat16),
        heads_of(values_all),
        preferred_element_type=jnp.float32,
    )
    mixed_low = mixed.reshape(local_rows, width).astype(jnp.bfloat16)
    columns = mixed_low
    base_out = jnp.dot(
        columns,
        lax.all_gather(attention_output_weight, "shard", axis=0, tiled=True),
        preferred_element_type=jnp.float32,
    )
    narrow_out = jnp.einsum(
        "td,rd->tr", mixed_low, a_one[3], preferred_element_type=jnp.float32
    ).astype(jnp.bfloat16)
    branch = base_out + jnp.dot(narrow_out, b_one[3], preferred_element_type=jnp.float32)
    middle = residual_in + BRANCH * branch
    normed_second = norm_rows(middle, gain_two).astype(jnp.bfloat16)
    narrow_mlp = jnp.einsum(
        "td,srd->str", normed_second, a_one[4:6], preferred_element_type=jnp.float32
    ).astype(jnp.bfloat16)
    lifted_mlp = jnp.einsum(
        "str,srf->stf", narrow_mlp, b_hidden_one, preferred_element_type=jnp.float32
    )
    columns = normed_second
    base_gate_up = jnp.einsum(
        "tr,srf->stf",
        columns,
        lax.all_gather(gate_up_projection_weight, "shard", axis=1, tiled=True),
        preferred_element_type=jnp.float32,
    )
    gate = base_gate_up[0] + lifted_mlp[0]
    up = base_gate_up[1] + lifted_mlp[1]
    hidden_low = (jax.nn.silu(gate) * up).astype(jnp.bfloat16)
    narrow_down = jnp.einsum(
        "tf,rf->tr", hidden_low, single_hidden_input_map, preferred_element_type=jnp.float32
    ).astype(jnp.bfloat16)
    columns = hidden_low
    base_down = jnp.dot(
        columns,
        lax.all_gather(down_projection_weight, "shard", axis=0, tiled=True),
        preferred_element_type=jnp.float32,
    )
    feed = base_down + jnp.dot(narrow_down, b_one[4], preferred_element_type=jnp.float32)
    output = (middle + BRANCH * feed).astype(jnp.bfloat16)
    grad_out = cotangent[0].astype(jnp.float32)
    grad_feed = (BRANCH * grad_out).astype(jnp.bfloat16)
    grad_b_down = jnp.einsum(
        "tr,td->rd", narrow_down, grad_feed, preferred_element_type=jnp.float32
    )
    down_lowrank_gradient = jnp.einsum(
        "td,rd->tr", grad_feed, b_one[4], preferred_element_type=jnp.float32
    ).astype(jnp.bfloat16)
    grad_a_down = jnp.einsum(
        "tr,tf->rf", down_lowrank_gradient, hidden_low, preferred_element_type=jnp.float32
    )
    adapter_hidden_output = jnp.dot(
        down_lowrank_gradient, single_hidden_input_map, preferred_element_type=jnp.float32
    )
    frozen_hidden_output = jnp.einsum(
        "td,rd->tr",
        grad_feed,
        lax.all_gather(down_projection_weight, "shard", axis=0, tiled=True),
        preferred_element_type=jnp.float32,
    )
    hidden_gradient = rounded_amount(frozen_hidden_output + adapter_hidden_output)
    _, silu_back = jax.vjp(lambda gate_in, up_in: jax.nn.silu(gate_in) * up_in, gate, up)
    grad_gate, grad_up = silu_back(hidden_gradient)
    stacked_mlp = jnp.stack([grad_gate.astype(jnp.bfloat16), grad_up.astype(jnp.bfloat16)])
    grad_b_mlp = jnp.einsum(
        "str,stf->srf", narrow_mlp, stacked_mlp, preferred_element_type=jnp.float32
    )
    grad_narrow_mlp = jnp.einsum(
        "stf,srf->str", stacked_mlp, b_hidden_one, preferred_element_type=jnp.float32
    ).astype(jnp.bfloat16)
    grad_a_mlp = jnp.einsum(
        "str,td->srd", grad_narrow_mlp, normed_second, preferred_element_type=jnp.float32
    )
    adapter_second_output = jnp.einsum(
        "str,srd->td", grad_narrow_mlp, a_one[4:6], preferred_element_type=jnp.float32
    )
    frozen_second_output = jnp.einsum(
        "stf,srf->tr",
        stacked_mlp,
        lax.all_gather(gate_up_projection_weight, "shard", axis=1, tiled=True),
        preferred_element_type=jnp.float32,
    )
    second_normed_gradient = frozen_second_output + adapter_second_output
    _, norm_back_second = jax.vjp(lambda values: norm_rows(values, gain_two), middle)
    grad_middle = grad_out + norm_back_second(second_normed_gradient)[0]
    grad_branch = (BRANCH * grad_middle).astype(jnp.bfloat16)
    grad_b_out = jnp.einsum(
        "tr,td->rd", narrow_out, grad_branch, preferred_element_type=jnp.float32
    )
    grad_narrow_out = jnp.einsum(
        "td,rd->tr", grad_branch, b_one[3], preferred_element_type=jnp.float32
    ).astype(jnp.bfloat16)
    grad_a_out = jnp.einsum(
        "tr,td->rd", grad_narrow_out, mixed_low, preferred_element_type=jnp.float32
    )
    base_mixed = jnp.einsum(
        "td,rd->tr",
        grad_branch,
        lax.all_gather(attention_output_weight, "shard", axis=0, tiled=True),
        preferred_element_type=jnp.float32,
    )
    grad_mixed = (
        base_mixed + jnp.dot(grad_narrow_out, a_one[3], preferred_element_type=jnp.float32)
    ).astype(jnp.bfloat16)
    probs_again = jnp.exp(attention_scores(query_turned, keys_all, visible) - log_total)
    grad_mixed_heads = heads_of(grad_mixed)
    grad_probs = jnp.einsum(
        "qhd,khd->hqk", grad_mixed_heads, heads_of(values_all), preferred_element_type=jnp.float32
    )
    inner = jnp.sum(grad_probs * probs_again, axis=-1, keepdims=True)
    grad_scores = (probs_again * (grad_probs - inner)).astype(jnp.bfloat16)
    scale = 1.0 / math.sqrt(HDIM)
    grad_query_turned = (
        jnp.einsum(
            "hqk,khd->qhd", grad_scores, heads_of(keys_all), preferred_element_type=jnp.float32
        ).reshape(local_rows, width)
        * scale
    )
    key_terms = (
        jnp.einsum(
            "hqk,qhd->khd", grad_scores, heads_of(query_turned), preferred_element_type=jnp.float32
        ).reshape(keys_all.shape[0], width)
        * scale
    )
    value_terms = jnp.einsum(
        "hqk,qhd->khd",
        probs_again.astype(jnp.bfloat16),
        grad_mixed_heads,
        preferred_element_type=jnp.float32,
    ).reshape(keys_all.shape[0], width)
    grad_key_turned, grad_value = (
        lax.psum_scatter(
            key_terms.astype(jnp.bfloat16), "shard", scatter_dimension=0, tiled=True
        ).astype(jnp.float32),
        lax.psum_scatter(
            value_terms.astype(jnp.bfloat16), "shard", scatter_dimension=0, tiled=True
        ).astype(jnp.float32),
    )
    _, turn_back = jax.vjp(lambda values: rotate(values, positions_local), empty)
    stacked_first = jnp.stack(
        [
            turn_back(grad_query_turned)[0].astype(jnp.bfloat16),
            turn_back(grad_key_turned)[0].astype(jnp.bfloat16),
            grad_value.astype(jnp.bfloat16),
        ]
    )
    grad_b_first = jnp.einsum(
        "str,std->srd", narrow_first, stacked_first, preferred_element_type=jnp.float32
    )
    grad_narrow_first = jnp.einsum(
        "std,srd->str", stacked_first, b_one[0:3], preferred_element_type=jnp.float32
    ).astype(jnp.bfloat16)
    grad_a_first = jnp.einsum(
        "str,td->srd", grad_narrow_first, normed, preferred_element_type=jnp.float32
    )
    base_normed = jnp.einsum(
        "std,srd->tr",
        stacked_first,
        lax.all_gather(query_key_value_weight, "shard", axis=1, tiled=True),
        preferred_element_type=jnp.float32,
    )
    grad_normed = base_normed + jnp.einsum(
        "str,srd->td", grad_narrow_first, a_one[0:3], preferred_element_type=jnp.float32
    )
    _, norm_back_first = jax.vjp(lambda values: norm_rows(values, gain_one), residual_in)
    input_grad = grad_middle + norm_back_first(grad_normed)[0]
    grad_a_model_one = jnp.concatenate([grad_a_first, grad_a_out[None], grad_a_mlp], axis=0)
    grad_b_model_one = jnp.concatenate([grad_b_first, grad_b_out[None], grad_b_down[None]], axis=0)
    per_processor_share = adapter_model_input_maps.shape[1]
    adapters_total = per_processor_share * group
    chosen = (jnp.arange(adapters_total, dtype=jnp.int32) == pick).astype(jnp.float32)[
        None, :, None, None
    ]
    spread_a_model = grad_a_model_one[:, None] * chosen
    spread_b_model = grad_b_model_one[:, None] * chosen
    spread_a_hidden = grad_a_down[None, None] * chosen
    spread_b_hidden = grad_b_mlp[:, None] * chosen
    owned = (
        lax.psum_scatter(
            spread_a_model.astype(jnp.bfloat16), "shard", scatter_dimension=1, tiled=True
        ).astype(jnp.float32),
        lax.psum_scatter(
            spread_b_model.astype(jnp.bfloat16), "shard", scatter_dimension=1, tiled=True
        ).astype(jnp.float32),
        lax.psum_scatter(
            spread_a_hidden.astype(jnp.bfloat16), "shard", scatter_dimension=1, tiled=True
        ).astype(jnp.float32),
        lax.psum_scatter(
            spread_b_hidden.astype(jnp.bfloat16), "shard", scatter_dimension=1, tiled=True
        ).astype(jnp.float32),
    )
    summed = (
        lax.psum(owned[0].astype(jnp.bfloat16), "rep").astype(jnp.float32),
        lax.psum(owned[1].astype(jnp.bfloat16), "rep").astype(jnp.float32),
        lax.psum(owned[2].astype(jnp.bfloat16), "rep").astype(jnp.float32),
        lax.psum(owned[3].astype(jnp.bfloat16), "rep").astype(jnp.float32),
    )
    return (output[None], input_grad[None], summed[0], summed[1], summed[2][0], summed[3])


def solution(mesh):
    in_specs = (
        P("rep", "shard", None),
        P("rep", "shard", None),
        P("rep"),
        P("rep", None),
        P(),
        P(),
        P(None, "shard", None),
        P("shard", None),
        P(None, "shard", None),
        P("shard", None),
        P(None, "shard", None, None),
        P(None, "shard", None, None),
        P("shard", None, None),
        P(None, "shard", None, None),
    )
    out_specs = (
        P("rep", "shard", None),
        P("rep", "shard", None),
        P(None, "shard", None, None),
        P(None, "shard", None, None),
        P("shard", None, None),
        P(None, "shard", None, None),
    )
    return jax.shard_map(shards, mesh=mesh, in_specs=in_specs, out_specs=out_specs, check_vma=False)
```

profile of v0, /device:TPU:0, one launch (start us, length us, event | category | flops | bytes accessed | tf_op | source)
XLA Modules:
  0.0 1554.4 jit_solution(16283073855144799213)
XLA Ops:
  14.0 29.6 %all-gather.14.cloned.1.call-done = bf16[6,8,16,2304]{3,2,0,1:T(8,128)(2,1)} async-done(((bf16[6,2,16,2304]{3,2,0,1:T(8,128)(2,1)}), bf16[6,8,16,2304]{3,2,0,1:T(8,128)(2,1)}) %all-gather.14.cloned.1.call-update) | async-done | bytes 3538960 | tf_op jit(solution)/shard_map/all_gather | solution.py:91
  45.1 28.1 %all-gather.16.cloned.1.call-done = bf16[5,8,16,2304]{3,2,0,1:T(8,128)(2,1)} async-done(((bf16[5,2,16,2304]{3,2,0,1:T(8,128)(2,1)}), bf16[5,8,16,2304]{3,2,0,1:T(8,128)(2,1)}) %all-gather.16.cloned.1.call-update) | async-done | bytes 2949136 | tf_op jit(solution)/shard_map/all_gather | solution.py:92
  78.2 188.6 %all-gather.12.cloned.1.call-done = bf16[3,2304,2304]{2,1,0:T(8,128)(2,1)} async-done(((bf16[3,576,2304]{2,1,0:T(8,128)(2,1)}), bf16[3,2304,2304]{2,1,0:T(8,128)(2,1)}) %all-gather.12.cloned.1.call-update) | async-done | bytes 31850512 | tf_op jit(solution)/shard_map/all_gather | solution.py:102
  266.8 8.7 fusion.30
  281.0 11.8 fusion.24
  295.9 9.1 fusion.25
  335.1 95.6 %all-gather.28.cloned.1.call-done = bf16[5760,2304]{1,0:T(8,128)(2,1)} async-done(((bf16[1440,2304]{1,0:T(8,128)(2,1)}), bf16[5760,2304]{1,0:T(8,128)(2,1)}) %all-gather.28.cloned.1.call-update) | async-done | bytes 26542096 | tf_op jit(solution)/shard_map/all_gather | solution.py:169
  430.7 15.2 fusion.93
  457.2 33.5 %all-gather.18.cloned.1.call-done = bf16[1024,2304]{1,0:T(8,128)(2,1)} async-done(((bf16[256,2304]{1,0:T(8,128)(2,1)}), bf16[1024,2304]{1,0:T(8,128)(2,1)}) %all-gather.18.cloned.1.call-update) | async-done | bytes 4718608 | tf_op jit(solution)/shard_map/all_gather | solution.py:120
  497.3 33.0 %all-gather.20.cloned.1.call-done = bf16[1024,2304]{1,0:T(8,128)(2,1)} async-done(((bf16[256,2304]{1,0:T(8,128)(2,1)}), bf16[1024,2304]{1,0:T(8,128)(2,1)}) %all-gather.20.cloned.1.call-update) | async-done | bytes 4718608 | tf_op jit(solution)/shard_map/all_gather | solution.py:119
  536.9 19.5 %fusion.6 = (f32[36,256]{1,0:T(8,128)S(1)}, f32[36,256,1024]{2,1,0:T(8,128)}) fusion(pred[256,1024]{1,0:T(8,128)(4,1)S(1)} %fusion.91, bf16[256,36,64]{0,2,1:T(8,128)(2,1)S(1)} %bitcast.303, bf16[1024,36,64]{0,2,1:T(8,128)(2,1)} %bitcast.298), kind=kOutput, calls=%fused_computation.11 | convolution fusion | flops 1236261888 | bytes 43945984 | tf_op jit(solution)/shard_map/qhd,khd->hqk/dot_general | solution.py:56
  556.4 17.5 %fusion = f32[36,256]{1,0:T(8,128)S(1)} fusion(f32[36,256]{1,0:T(8,128)S(1)} %get-tuple-element.39, f32[36,256,1024]{2,1,0:T(8,128)} %get-tuple-element.40, pred[256,1024]{1,0:T(8,128)(4,1)S(1)} %fusion.91), kind=kLoop, calls=%fused_computation.6 | loop fusion | flops 37739520 | bytes 38084608 | tf_op jit(solution)/shard_map/reduce_sum | solution.py:125
  574.0 15.9 %fusion.65 = bf16[36,64,256]{2,1,0:T(8,128)(2,1)S(1)} fusion(bf16[1024,36,64]{0,2,1:T(8,128)(2,1)S(1)} %bitcast.301, f32[36,256]{1,0:T(8,128)S(1)} %fusion, f32[36,256]{1,0:T(8,128)S(1)} %get-tuple-element.39, f32[36,256,1024]{2,1,0:T(8,128)} %get-tuple-element.40, pred[256,1024]{1,0:T(8,128)(4,1)S(1)} %fusion.91), kind=kOutput, calls=%fused_computation.121 | convolution fusion | flops 1255735296 | bytes 43982848 | tf_op jit(solution)/shard_map/hqk,khd->qhd/dot_general | solution.py:128
  591.8 11.1 all-gather.22.cloned.1.call-done
  614.0 17.9 %all-gather.26.cloned.1.call-done = bf16[2,8,16,5760]{3,2,1,0:T(8,128)(2,1)} async-done(((bf16[2,2,16,5760]{3,2,1,0:T(8,128)(2,1)}), bf16[2,8,16,5760]{3,2,1,0:T(8,128)(2,1)}) %all-gather.26.cloned.1.call-update) | async-done | bytes 2949136 | tf_op jit(solution)/shard_map/all_gather | solution.py:94
  638.9 308.1 %all-gather.24.cloned.1.call-done = bf16[2,2304,5760]{2,1,0:T(8,128)(2,1)} async-done(((bf16[2,576,5760]{2,1,0:T(8,128)(2,1)}), bf16[2,2304,5760]{2,1,0:T(8,128)(2,1)}) %all-gather.24.cloned.1.call-update) | async-done | bytes 53084176 | tf_op jit(solution)/shard_map/all_gather | solution.py:157
  947.0 26.5 %convolution_bitcast_fusion = f32[2,256,5760]{2,1,0:T(8,128)} fusion(bf16[256,2304,1]{1,0,2:T(8,128)(2,1)S(1)} %fusion.66, bf16[2,2304,5760]{2,1,0:T(8,128)(2,1)} %all-gather.24.cloned.1.call-done), kind=kOutput, calls=%fused_computation.18 | convolution fusion | flops 13589544960 | bytes 66060288 | tf_op jit(solution)/shard_map/tr,srf->stf/dot_general | solution.py:154
  973.5 13.2 fusion.43
  987.9 7.3 fusion.34
  995.1 24.0 %convolution_bitcast_fusion.2 = f32[256,2304]{1,0:T(8,128)} fusion(bf16[2,2304,5760]{2,1,0:T(8,128)(2,1)} %all-gather.24.cloned.1.call-done, bf16[1,256,5760]{2,1,0:T(8,128)(2,1)} %get-tuple-element.17, bf16[1,256,5760]{2,1,0:T(8,128)(2,1)} %get-tuple-element.13), kind=kOutput, calls=%fused_computation.55 | convolution fusion | flops 13592494080 | bytes 61341696 | tf_op jit(solution)/shard_map/stf,srf->tr/dot_general | solution.py:210
  1033.3 29.5 %multiply_reduce_fusion = (f32[36,256]{1,0:T(8,128)S(1)}, f32[36,256,1024]{2,1,0:T(8,128)}) fusion(f32[36,256]{1,0:T(8,128)S(1)} %copy-done.34, f32[36,256,1024]{2,1,0:T(8,128)} %get-tuple-element.40, pred[256,1024]{1,0:T(8,128)(4,1)S(1)} %copy-done.18, bf16[256,36,64]{0,2,1:T(8,128)(2,1)S(1)} %bitcast.315, bf16[1024,36,64]{0,2,1:T(8,128)(2,1)} %bitcast.300), kind=kOutput, calls=%fused_computation.1 | convolution fusion | flops 1255136256 | bytes 81731584 | tf_op jit(solution)/shard_map/qhd,khd->hqk/dot_general | solution.py:240
  1062.8 31.5 %multiply_convert_fusion = bf16[36,256,1024]{2,1,0:T(8,128)(2,1)} fusion(f32[36,256,1024]{2,1,0:T(8,128)} %get-tuple-element.46, f32[36,256]{1,0:T(8,128)S(1)} %get-tuple-element.45, f32[36,256]{1,0:T(8,128)S(1)} %copy-done.34, f32[36,256,1024]{2,1,0:T(8,128)} %get-tuple-element.40, pred[256,1024]{1,0:T(8,128)(4,1)S(1)} %copy-done.18), kind=kLoop, calls=%fused_computation | loop fusion | flops 56623104 | bytes 94707712 | tf_op jit(solution)/shard_map/convert_element_type | solution.py:244
  1094.3 12.0 multiply_convert_fusion.1
  1106.4 21.0 %fusion.44 = bf16[36,64,1024]{2,1,0:T(8,128)(2,1)} fusion(bf16[256,36,64]{0,2,1:T(8,128)(2,1)S(1)} %bitcast.316, f32[36,256]{1,0:T(8,128)S(1)} %copy-done.34, f32[36,256,1024]{2,1,0:T(8,128)} %get-tuple-element.40, pred[256,1024]{1,0:T(8,128)(4,1)S(1)} %copy-done.18), kind=kOutput, calls=%fused_computation.89 | convolution fusion | flops 1248067584 | bytes 43945984 | tf_op jit(solution)/shard_map/hqk,qhd->khd/dot_general | solution.py:258
  1134.9 11.0 bitcast_multiply_fusion.3
  1149.8 7.9 fusion.88
  1168.7 36.1 %reduce-scatter.15.cloned.1.call-done = bf16[256,2304]{1,0:T(8,128)(2,1)} async-done(((bf16[1024,2304]{1,0:T(8,128)(2,1)}), bf16[256,2304]{1,0:T(8,128)(2,1)}) %reduce-scatter.15.cloned.1.call-update) | async-done | bytes 1179664 | tf_op jit(solution)/shard_map/reduce_scatter | solution.py:268
  1220.5 13.7 fusion.147
  1236.6 148.9 %all-reduce.14.cloned.1.call-done = (bf16[6,8,16,2304]{3,2,1,0:T(8,128)(2,1)}, bf16[5,8,16,2304]{3,2,1,0:T(8,128)(2,1)}, bf16[2,8,16,5760]{3,2,1,0:T(8,128)(2,1)}) async-done(((bf16[6,8,16,2304]{3,2,1,0:T(8,128)(2,1)}, bf16[5,8,16,2304]{3,2,1,0:T(8,128)(2,1)}, bf16[2,8,16,5760]{3,2,1,0:T(8,128)(2,1)}), (bf16[6,8,16,2304]{3,2,1,0:T(8,128)(2,1)}, bf16[5,8,16,2304]{3,2,1,0:T(8,128)(2,1)}, ...) | async-done | bytes 9437200
  1391.9 24.4 %reduce-scatter.17.cloned.1.call-done = bf16[1,2,16,5760]{3,2,1,0:T(8,128)(2,1)} async-done(((bf16[1,8,16,5760]{3,2,1,0:T(8,128)(2,1)}), bf16[1,2,16,5760]{3,2,1,0:T(8,128)(2,1)}) %reduce-scatter.17.cloned.1.call-update) | async-done | bytes 368656 | tf_op jit(solution)/shard_map/reduce_scatter | solution.py:318
  1416.3 15.4 convolution_bitcast_fusion.1
  1435.5 105.1 %all-reduce.12.cloned.1.call-done = (bf16[6,2,16,2304]{3,2,1,0:T(8,128)(2,1)}, bf16[5,2,16,2304]{3,2,1,0:T(8,128)(2,1)}, bf16[2,16,5760]{2,1,0:T(8,128)(2,1)}, bf16[2,2,16,5760]{3,2,1,0:T(8,128)(2,1)}) async-done(((bf16[6,2,16,2304]{3,2,1,0:T(8,128)(2,1)}, bf16[5,2,16,2304]{3,2,1,0:T(8,128)(2,1)}, bf16[2,16,5760]{2,1,0:T(8,128)(2,1)}, bf16[2,2,16,5760]{3,2,1,0:T(8,128)(2,1)}), ...) | async-done | bytes 2727952 | tf_op jit(solution)/shard_map/psum | solution.py:326
  (270 shorter events, 166.1 us)
Async XLA Ops:
  7.2 36.5 %all-gather.14.cloned.1.call-start = ((), (), s32[]{:S(2)}) async-start(), calls=%async_computation.4 | async-start | bytes 4423680 | tf_op jit(solution)/shard_map/all_gather | solution.py:91
  9.4 63.8 %all-gather.16.cloned.1.call-start = ((), (), s32[]{:S(2)}) async-start(), calls=%async_computation.5 | async-start | bytes 3686400 | tf_op jit(solution)/shard_map/all_gather | solution.py:92
  10.4 256.3 %all-gather.12.cloned.1.call-start = ((), (), s32[]{:S(2)}) async-start(), calls=%async_computation.3 | async-start | bytes 39813120 | tf_op jit(solution)/shard_map/all_gather | solution.py:102
  11.2 419.5 %all-gather.28.cloned.1.call-start = ((), (), s32[]{:S(2)}) async-start(), calls=%async_computation.11 | async-start | bytes 33177600 | tf_op jit(solution)/shard_map/all_gather | solution.py:169
  11.8 439.4 %all-gather.30.cloned.1.call-start = ((), (), s32[]{:S(2)}) async-start(), calls=%async_computation.15 | async-start | bytes 1843200 | tf_op jit(solution)/shard_map/all_gather | solution.py:93
  12.4 478.3 %all-gather.18.cloned.1.call-start = ((), (), s32[]{:S(2)}) async-start(), calls=%async_computation.6 | async-start | bytes 5898240 | tf_op jit(solution)/shard_map/all_gather | solution.py:120
  13.1 282.9 %copy-start.53 = (f32[2304]{0:T(1024)}, f32[2304]{0:T(1024)S(1)}, u32[]{:S(2)}) copy-start(f32[2304]{0:T(1024)S(1)} %convert_element_type.235) | copy-start | bytes 27652
  14.0 281.9 %copy-start.68 = (f32[256]{0:T(256)}, f32[256]{0:T(256)S(1)}, u32[]{:S(2)}) copy-start(f32[256]{0:T(256)S(1)} %fusion.123) | copy-start | bytes 3076
  45.1 33.1 %copy-start.61 = (bf16[3,16,256]{2,1,0:T(8,128)(2,1)}, bf16[3,16,256]{2,1,0:T(8,128)(2,1)S(1)}, u32[]{:S(2)}) copy-start(bf16[3,16,256]{2,1,0:T(8,128)(2,1)S(1)} %fusion.81) | copy-start | bytes 73732
  275.5 254.9 %all-gather.20.cloned.1.call-start = ((), (), s32[]{:S(2)}) async-start(), calls=%async_computation.7 | async-start | bytes 5898240 | tf_op jit(solution)/shard_map/all_gather | solution.py:119
  326.1 276.7 %all-gather.22.cloned.1.call-start = ((), (), s32[]{:S(2)}) async-start(), calls=%async_computation.8 | async-start | bytes 13271040 | tf_op jit(solution)/shard_map/all_gather | solution.py:138
  326.9 305.0 %all-gather.26.cloned.1.call-start = ((), (), s32[]{:S(2)}) async-start(), calls=%async_computation.10 | async-start | bytes 3686400 | tf_op jit(solution)/shard_map/all_gather | solution.py:94
  327.7 619.3 %all-gather.24.cloned.1.call-start = ((), (), s32[]{:S(2)}) async-start(), calls=%async_computation.9 | async-start | bytes 66355200 | tf_op jit(solution)/shard_map/all_gather | solution.py:157
  328.3 835.9 %reduce-scatter.13.cloned.1.call-start = ((), (), s32[]{:S(2)}) async-start(), calls=%async_computation.12 | async-start | bytes 5898240 | tf_op jit(solution)/shard_map/reduce_scatter | solution.py:265
  333.7 240.3 %copy-start.17 = (pred[256,1024]{1,0:T(8,128)(4,1)}, pred[256,1024]{1,0:T(8,128)(4,1)S(1)}, u32[]{:S(2)}) copy-start(pred[256,1024]{1,0:T(8,128)(4,1)S(1)} %fusion.91) | copy-start | bytes 786436
  335.1 116.1 %copy-start.55 = (bf16[256,16]{0,1:T(8,128)(2,1)}, bf16[256,16]{0,1:T(8,128)(2,1)S(1)}, u32[]{:S(2)}) copy-start(bf16[256,16]{0,1:T(8,128)(2,1)S(1)} %fusion.85) | copy-start | bytes 24580
  457.2 79.8 %copy-start.8 = (bf16[256,2304]{0,1:T(8,128)(2,1)}, bf16[256,2304]{0,1:T(8,128)(2,1)S(1)}, u32[]{:S(2)}) copy-start(bf16[256,2304]{0,1:T(8,128)(2,1)S(1)} %copy.56) | copy-start | bytes 3538948
  556.4 17.6 %copy-start.43 = (f32[36,256]{1,0:T(8,128)}, f32[36,256]{1,0:T(8,128)S(1)}, u32[]{:S(2)}) copy-start(f32[36,256]{1,0:T(8,128)S(1)} %get-tuple-element.39) | copy-start | bytes 110596
  556.4 17.6 %copy-start.6 = (bf16[1024,2304]{0,1:T(8,128)(2,1)S(1)}, bf16[1024,2304]{0,1:T(8,128)(2,1)}, u32[]{:S(2)}) copy-start(bf16[1024,2304]{0,1:T(8,128)(2,1)} %copy.52) | copy-start | bytes 14155780
  591.8 17.2 %copy-start.11 = (bf16[1,256,2304]{2,1,0:T(8,128)(2,1)S(1)}, bf16[1,256,2304]{2,1,0:T(8,128)(2,1)}, u32[]{:S(2)}) copy-start(bf16[1,256,2304]{2,1,0:T(8,128)(2,1)} %param.14) | copy-start | bytes 3538948
  610.7 414.6 %copy-start.1 = (f32[256,2304]{1,0:T(8,128)}, f32[256,2304]{1,0:T(8,128)S(1)}, u32[]{:S(2)}) copy-start(f32[256,2304]{1,0:T(8,128)S(1)} %get-tuple-element.42) | copy-start | bytes 7077892
  611.7 335.3 %copy-start.13 = (bf16[256,2304,1]{1,0,2:T(8,128)(2,1)}, bf16[256,2304,1]{1,0,2:T(8,128)(2,1)S(1)}, u32[]{:S(2)}) copy-start(bf16[256,2304,1]{1,0,2:T(8,128)(2,1)S(1)} %fusion.66) | copy-start | bytes 3538948
  947.0 26.5 %copy-start.7 = (bf16[256,5760]{1,0:T(8,128)(2,1)S(1)}, bf16[256,5760]{1,0:T(8,128)(2,1)}, u32[]{:S(2)}) copy-start(bf16[256,5760]{1,0:T(8,128)(2,1)} %fusion.10) | copy-start | bytes 8847364
  995.1 24.0 %copy-start.24 = (bf16[1,256,5760]{2,1,0:T(8,128)(2,1)S(1)}, bf16[1,256,5760]{2,1,0:T(8,128)(2,1)}, u32[]{:S(2)}) copy-start(bf16[1,256,5760]{2,1,0:T(8,128)(2,1)} %get-tuple-element.17) | copy-start | bytes 8847364
  1062.8 31.6 %copy-start.9 = (bf16[256,2304]{0,1:T(8,128)(2,1)S(1)}, bf16[256,2304]{0,1:T(8,128)(2,1)}, u32[]{:S(2)}) copy-start(bf16[256,2304]{0,1:T(8,128)(2,1)} %copy-done.8) | copy-start | bytes 3538948
  1106.3 98.5 %reduce-scatter.15.cloned.1.call-start = ((), (), s32[]{:S(2)}) async-start(), calls=%async_computation.13 | async-start | bytes 5898240 | tf_op jit(solution)/shard_map/reduce_scatter | solution.py:268
  1134.1 251.5 %all-reduce.14.cloned.1.call-start = ((), (), s32[]{:S(2)}) async-start(), calls=%async_computation.17 | async-start | bytes 18874368
  1148.7 56.1 %copy-start.27 = (bf16[1,256,2304]{2,1,0:T(8,128)(2,1)}, bf16[1,256,2304]{2,1,0:T(8,128)(2,1)S(1)}, u32[]{:S(2)}) copy-start(bf16[1,256,2304]{2,1,0:T(8,128)(2,1)S(1)} %copy.63) | copy-start | bytes 3538948
  1168.7 38.2 %copy-start.29 = (bf16[1,256,2304]{2,1,0:T(8,128)(2,1)}, bf16[1,256,2304]{2,1,0:T(8,128)(2,1)S(1)}, u32[]{:S(2)}) copy-start(bf16[1,256,2304]{2,1,0:T(8,128)(2,1)S(1)} %copy.64) | copy-start | bytes 3538948
  1214.8 201.4 %reduce-scatter.17.cloned.1.call-start = ((), (), s32[]{:S(2)}) async-start(), calls=%async_computation.14 | async-start | bytes 1843200 | tf_op jit(solution)/shard_map/reduce_scatter | solution.py:318
  1220.4 320.2 %all-reduce.12.cloned.1.call-start = ((), (), s32[]{:S(2)}) async-start(), calls=%async_computation.16 | async-start | bytes 5455872 | tf_op jit(solution)/shard_map/psum | solution.py:326
  1389.7 26.6 %copy-start.28 = (bf16[1,256,2304]{2,1,0:T(8,128)(2,1)S(1)}, bf16[1,256,2304]{2,1,0:T(8,128)(2,1)}, u32[]{:S(2)}) copy-start(bf16[1,256,2304]{2,1,0:T(8,128)(2,1)} %copy-done.27) | copy-start | bytes 3538948
  (60 other events, 264.0 us)
Sparse Core Ops, SparseCore 0:
  10.1 33.4 all-gather.13
  45.8 27.4 all-gather.15
  74.8 191.9 all-gather.11
  268.2 162.4 all-gather.27
  432.1 19.0 all-gather.29
  453.2 37.4 all-gather.17
  492.8 37.4 all-gather.19
  531.9 70.9 all-gather.21
  604.4 27.4 all-gather.25
  633.3 313.6 all-gather.23
  1106.4 47.8 reduce-scatter.12
  1156.9 47.8 reduce-scatter.14
  1215.0 170.5 all-reduce.13
  1388.6 27.6 reduce-scatter.16
  1421.2 119.4 all-reduce.11
where the time goes:
time: 1560 us; the launch traced here: 1550 us
  waiting for transfers between devices  1070 us (69%)
  matrix products  302 us (19%)
  other arithmetic  108 us (7%)
  local copies, waits for them, and re-layouts  56.9 us (4%)
  between operations  17.8 us (1%)
    all_gather x1, waiting for transfers between devices, shards(): lax.all_gather(gate_up_projection_weight, 'shard', axis=1, tiled=True)  308 us
    all_gather x1, waiting for transfers between devices, shards(): pieces = lax.all_gather(query_key_value_weight, 'shard', axis=1, tiled=True)  189 us
    unnamed x16, waiting for transfers between devices  153 us
    psum x1, waiting for transfers between devices, shards(): lax.psum(owned[0].astype(jnp.bfloat16), 'rep').astype(jnp.float32)  105 us
    all_gather x1, waiting for transfers between devices, shards(): lax.all_gather(down_projection_weight, 'shard', axis=0, tiled=True)  95.6 us
    reduce_scatter x1, waiting for transfers between devices, shards(): lax.psum_scatter(value_terms.astype(jnp.bfloat16), 'shard', scatter_dimen...  36.1 us
    all_gather x1, waiting for transfers between devices, shards(): lax.all_gather(value_low, 'shard', axis=0, tiled=True)  33.5 us
    all_gather x1, waiting for transfers between devices, shards(): lax.all_gather(key_turned, 'shard', axis=0, tiled=True)  33 us
  transfers between devices with their start and end apart: 15, of which 14 were waited for; matrix products, arithmetic and copies ran while one was open for 18% of the time, Pallas kernels for 0%

commit v1 on v0

--- a/solution.py
+++ b/solution.py
@@ -99,7 +99,14 @@
     b_hidden_one = lax.dynamic_index_in_dim(b_hidden_all, pick, 1, keepdims=False)
     normed = norm_rows(residual_in, gain_one).astype(jnp.bfloat16)
     empty = jnp.zeros((local_rows, width), jnp.float32)
-    pieces = lax.all_gather(query_key_value_weight, "shard", axis=1, tiled=True)
+    ring = [query_key_value_weight]
+    for hop in range(3):
+        ring.append(lax.ppermute(ring[-1], "shard", [(dev, (dev + 1) % 4) for dev in range(4)]))
+    pieces = jnp.roll(
+        jnp.concatenate(ring[::-1], axis=1),
+        (lax.axis_index("shard") + 1) * ring[0].shape[1],
+        axis=1,
+    )
     columns = normed
     base_query, base_key, base_value = tuple(
         (jnp.dot(columns, pieces[slot], preferred_element_type=jnp.float32) for slot in range(3))

time: 1560 us -> 1870 us (1.20)
  waiting for transfers between devices: 1070 us -> 1320 us
  local copies, waits for them, and re-layouts: 56.9 us -> 107 us
    ppermute x0 -> x3, waiting for transfers between devices: none -> 255 us  [shards(): lax.ppermute(ring[-1], 'shard', [(dev, (dev + 1) % 4) for dev in range(4)])]
    all_gather x1, waiting for transfers between devices: 95.6 us -> 157 us  [shards(): lax.all_gather(down_projection_weight, 'shard', axis=0, tiled=True)]
    unnamed x160 -> x163, local copies, waits for them, and re-layouts: 16.6 us -> 61.9 us
    all_gather x1, waiting for transfers between devices: 33.5 us -> 0.02 us  [shards(): lax.all_gather(value_low, 'shard', axis=0, tiled=True)]
    all_gather x1, waiting for transfers between devices: 29.6 us -> 0.01 us  [shards(): lax.all_gather(adapter_model_input_maps, 'shard', axis=1, tiled=True)]
  transfers between devices with their start and end apart: 15 -> 18, of which waited for: 14 -> 15; matrix products, arithmetic and copies ran while one was open for 18% -> 15% of each run, Pallas kernels for 0% -> 0%
where the time goes in v1:
time: 1870 us; the launch traced here: 1860 us
  waiting for transfers between devices  1320 us (71%)
  matrix products  309 us (17%)
  local copies, waits for them, and re-layouts  107 us (6%)
  other arithmetic  106 us (6%)
    all_gather x1, waiting for transfers between devices, shards(): lax.all_gather(gate_up_projection_weight, 'shard', axis=1, tiled=True)  310 us
    ppermute x3, waiting for transfers between devices, shards(): lax.ppermute(ring[-1], 'shard', [(dev, (dev + 1) % 4) for dev in range(4)])  255 us
    all_gather x1, waiting for transfers between devices, shards(): lax.all_gather(query_key_value_weight, 'shard', axis=1, tiled=True)  193 us
    all_gather x1, waiting for transfers between devices, shards(): lax.all_gather(down_projection_weight, 'shard', axis=0, tiled=True)  157 us
    unnamed x16, waiting for transfers between devices  153 us
    psum x1, waiting for transfers between devices, shards(): lax.psum(owned[0].astype(jnp.bfloat16), 'rep').astype(jnp.float32)  103 us
    unnamed x163, local copies, waits for them, and re-layouts  61.9 us
  transfers between devices with their start and end apart: 18, of which 15 were waited for; matrix products, arithmetic and copies ran while one was open for 15% of the time, Pallas kernels for 0%

profile of v1, /device:TPU:0, one launch (start us, length us, event | category | flops | bytes accessed | tf_op | source)
XLA Modules:
  0.0 1863.7 jit_solution(6999120107989978421)
XLA Ops:
  7.7 88.8 %collective-permute-done = bf16[3,576,2304]{2,1,0:T(8,128)(2,1)} collective-permute-done((bf16[3,576,2304]{2,1,0:T(8,128)(2,1)}, bf16[3,576,2304]{2,1,0:T(8,128)(2,1)}, u32[]{:S(2)}, u32[]{:S(2)}) %collective-permute-start) | collective-permute-done | bytes 7962656 | tf_op jit(solution)/shard_map/ppermute | solution.py:104
  98.8 105.4 %collective-permute-done.1 = bf16[3,576,2304]{2,1,0:T(8,128)(2,1)} collective-permute-done((bf16[3,576,2304]{2,1,0:T(8,128)(2,1)}, bf16[3,576,2304]{2,1,0:T(8,128)(2,1)}, u32[]{:S(2)}, u32[]{:S(2)}) %collective-permute-start.1) | collective-permute-done | bytes 7962656 | tf_op jit(solution)/shard_map/ppermute | solution.py:104
  208.3 34.7 %all-gather.14.cloned.1.call-done = bf16[5,8,16,2304]{3,2,0,1:T(8,128)(2,1)} async-done(((bf16[5,2,16,2304]{3,2,0,1:T(8,128)(2,1)}), bf16[5,8,16,2304]{3,2,0,1:T(8,128)(2,1)}) %all-gather.14.cloned.1.call-update) | async-done | bytes 2949136 | tf_op jit(solution)/shard_map/all_gather | solution.py:92
  247.9 60.7 %collective-permute-done.2 = bf16[3,576,2304]{2,1,0:T(8,128)(2,1)} collective-permute-done((bf16[3,576,2304]{2,1,0:T(8,128)(2,1)}, bf16[3,576,2304]{2,1,0:T(8,128)(2,1)}, u32[]{:S(2)}, u32[]{:S(2)}) %collective-permute-start.2) | collective-permute-done | bytes 7962656 | tf_op jit(solution)/shard_map/ppermute | solution.py:104
  358.1 9.3 fusion.30
  372.3 12.7 fusion.29
  388.2 12.3 fusion.28
  439.9 21.5 %all-gather.18.cloned.1.call-done = bf16[1024,2304]{1,0:T(8,128)(2,1)} async-done(((bf16[256,2304]{1,0:T(8,128)(2,1)}), bf16[1024,2304]{1,0:T(8,128)(2,1)}) %all-gather.18.cloned.1.call-update) | async-done | bytes 4718608 | tf_op jit(solution)/shard_map/all_gather | solution.py:126
  468.0 19.3 %fusion.6 = (f32[36,256]{1,0:T(8,128)S(1)}, f32[36,256,1024]{2,1,0:T(8,128)}) fusion(pred[256,1024]{1,0:T(8,128)(4,1)S(1)} %fusion.91, bf16[256,36,64]{0,2,1:T(8,128)(2,1)S(1)} %bitcast.305, bf16[1024,36,64]{0,2,1:T(8,128)(2,1)} %bitcast.298), kind=kOutput, calls=%fused_computation.11 | convolution fusion | flops 1236261888 | bytes 43945984 | tf_op jit(solution)/shard_map/qhd,khd->hqk/dot_general | solution.py:56
  487.3 17.5 fusion
  504.9 15.9 fusion.65
  522.7 11.1 all-gather.20.cloned.1.call-done
  545.2 17.5 all-gather.24.cloned.1.call-done
  569.6 157.1 %all-gather.26.cloned.1.call-done = bf16[5760,2304]{1,0:T(8,128)(2,1)} async-done(((bf16[1440,2304]{1,0:T(8,128)(2,1)}), bf16[5760,2304]{1,0:T(8,128)(2,1)}) %all-gather.26.cloned.1.call-update) | async-done | bytes 26542096 | tf_op jit(solution)/shard_map/all_gather | solution.py:176
  726.7 14.5 fusion.93
  752.8 309.9 %all-gather.22.cloned.1.call-done = bf16[2,2304,5760]{2,1,0:T(8,128)(2,1)} async-done(((bf16[2,576,5760]{2,1,0:T(8,128)(2,1)}), bf16[2,2304,5760]{2,1,0:T(8,128)(2,1)}) %all-gather.22.cloned.1.call-update) | async-done | bytes 53084176 | tf_op jit(solution)/shard_map/all_gather | solution.py:164
  1062.7 26.4 %convolution_bitcast_fusion = f32[2,256,5760]{2,1,0:T(8,128)} fusion(bf16[256,2304,1]{1,0,2:T(8,128)(2,1)S(1)} %fusion.66, bf16[2,2304,5760]{2,1,0:T(8,128)(2,1)} %all-gather.22.cloned.1.call-done), kind=kOutput, calls=%fused_computation.18 | convolution fusion | flops 13589544960 | bytes 66060288 | tf_op jit(solution)/shard_map/tr,srf->stf/dot_general | solution.py:161
  1089.1 13.2 fusion.43
  1110.8 23.9 %convolution_bitcast_fusion.2 = f32[256,2304]{1,0:T(8,128)} fusion(bf16[2,2304,5760]{2,1,0:T(8,128)(2,1)} %all-gather.22.cloned.1.call-done, bf16[1,256,5760]{2,1,0:T(8,128)(2,1)} %get-tuple-element.17, bf16[1,256,5760]{2,1,0:T(8,128)(2,1)} %get-tuple-element.13), kind=kOutput, calls=%fused_computation.52 | convolution fusion | flops 13592494080 | bytes 61341696 | tf_op jit(solution)/shard_map/stf,srf->tr/dot_general | solution.py:217
  1148.9 29.5 %multiply_reduce_fusion = (f32[36,256]{1,0:T(8,128)S(1)}, f32[36,256,1024]{2,1,0:T(8,128)}) fusion(f32[36,256]{1,0:T(8,128)S(1)} %copy-done.33, f32[36,256,1024]{2,1,0:T(8,128)} %get-tuple-element.40, pred[256,1024]{1,0:T(8,128)(4,1)S(1)} %copy-done.18, bf16[256,36,64]{0,2,1:T(8,128)(2,1)S(1)} %bitcast.317, bf16[1024,36,64]{0,2,1:T(8,128)(2,1)} %bitcast.302), kind=kOutput, calls=%fused_computation.1 | convolution fusion | flops 1255136256 | bytes 81731584 | tf_op jit(solution)/shard_map/qhd,khd->hqk/dot_general | solution.py:247
  1178.4 31.2 %multiply_convert_fusion = bf16[36,256,1024]{2,1,0:T(8,128)(2,1)} fusion(f32[36,256,1024]{2,1,0:T(8,128)} %get-tuple-element.46, f32[36,256]{1,0:T(8,128)S(1)} %get-tuple-element.45, f32[36,256]{1,0:T(8,128)S(1)} %copy-done.33, f32[36,256,1024]{2,1,0:T(8,128)} %get-tuple-element.40, pred[256,1024]{1,0:T(8,128)(4,1)S(1)} %copy-done.18), kind=kLoop, calls=%fused_computation | loop fusion | flops 56623104 | bytes 94707712 | tf_op jit(solution)/shard_map/convert_element_type | solution.py:251
  1209.7 11.9 multiply_convert_fusion.1
  1221.6 21.0 %fusion.44 = bf16[36,64,1024]{2,1,0:T(8,128)(2,1)} fusion(bf16[256,36,64]{0,2,1:T(8,128)(2,1)S(1)} %bitcast.318, f32[36,256]{1,0:T(8,128)S(1)} %copy-done.33, f32[36,256,1024]{2,1,0:T(8,128)} %get-tuple-element.40, pred[256,1024]{1,0:T(8,128)(4,1)S(1)} %copy-done.18), kind=kOutput, calls=%fused_computation.89 | convolution fusion | flops 1248067584 | bytes 43945984 | tf_op jit(solution)/shard_map/hqk,qhd->khd/dot_general | solution.py:265
  1250.1 11.3 bitcast_multiply_fusion.3
  1265.5 7.9 fusion.88
  1285.0 35.2 %reduce-scatter.15.cloned.1.call-done = bf16[256,2304]{1,0:T(8,128)(2,1)} async-done(((bf16[1024,2304]{1,0:T(8,128)(2,1)}), bf16[256,2304]{1,0:T(8,128)(2,1)}) %reduce-scatter.15.cloned.1.call-update) | async-done | bytes 1179664 | tf_op jit(solution)/shard_map/reduce_scatter | solution.py:275
  1337.2 13.5 fusion.150
  1353.2 149.0 %all-reduce.14.cloned.1.call-done = (bf16[6,8,16,2304]{3,2,1,0:T(8,128)(2,1)}, bf16[5,8,16,2304]{3,2,1,0:T(8,128)(2,1)}, bf16[2,8,16,5760]{3,2,1,0:T(8,128)(2,1)}) async-done(((bf16[6,8,16,2304]{3,2,1,0:T(8,128)(2,1)}, bf16[5,8,16,2304]{3,2,1,0:T(8,128)(2,1)}, bf16[2,8,16,5760]{3,2,1,0:T(8,128)(2,1)}), (bf16[6,8,16,2304]{3,2,1,0:T(8,128)(2,1)}, bf16[5,8,16,2304]{3,2,1,0:T(8,128)(2,1)}, ...) | async-done | bytes 9437200
  1508.4 24.6 %reduce-scatter.17.cloned.1.call-done = bf16[1,2,16,5760]{3,2,1,0:T(8,128)(2,1)} async-done(((bf16[1,8,16,5760]{3,2,1,0:T(8,128)(2,1)}), bf16[1,2,16,5760]{3,2,1,0:T(8,128)(2,1)}) %reduce-scatter.17.cloned.1.call-update) | async-done | bytes 368656 | tf_op jit(solution)/shard_map/reduce_scatter | solution.py:325
  1533.1 193.5 %all-gather.28.cloned.1.call-done = bf16[3,2304,2304]{2,1,0:T(8,128)(2,1)} async-done(((bf16[3,576,2304]{2,1,0:T(8,128)(2,1)}), bf16[3,2304,2304]{2,1,0:T(8,128)(2,1)}) %all-gather.28.cloned.1.call-update) | async-done | bytes 31850512 | tf_op jit(solution)/shard_map/all_gather | solution.py:299
  1726.5 17.0 convolution_bitcast_fusion.1
  1748.0 102.9 %all-reduce.12.cloned.1.call-done = (bf16[6,2,16,2304]{3,2,1,0:T(8,128)(2,1)}, bf16[5,2,16,2304]{3,2,1,0:T(8,128)(2,1)}, bf16[2,16,5760]{2,1,0:T(8,128)(2,1)}, bf16[2,2,16,5760]{3,2,1,0:T(8,128)(2,1)}) async-done(((bf16[6,2,16,2304]{3,2,1,0:T(8,128)(2,1)}, bf16[5,2,16,2304]{3,2,1,0:T(8,128)(2,1)}, bf16[2,16,5760]{2,1,0:T(8,128)(2,1)}, bf16[2,2,16,5760]{3,2,1,0:T(8,128)(2,1)}), ...) | async-done | bytes 2727952 | tf_op jit(solution)/shard_map/psum | solution.py:333
  (281 shorter events, 225.8 us)
Async XLA Ops:
  7.2 197.0 %copy-start.30 = (bf16[5,2,16,2304]{3,2,1,0:T(8,128)(2,1)S(1)}, bf16[5,2,16,2304]{3,2,1,0:T(8,128)(2,1)}, u32[]{:S(2)}) copy-start(bf16[5,2,16,2304]{3,2,1,0:T(8,128)(2,1)} %param.25) | copy-start | bytes 2211844
  7.2 198.6 %copy-start.62 = (bf16[2304]{0:T(1024)(128)(2,1)S(1)}, bf16[2304]{0:T(1024)(128)(2,1)}, u32[]{:S(2)}) copy-start(bf16[2304]{0:T(1024)(128)(2,1)} %param.18) | copy-start | bytes 13828
  7.2 198.7 %copy-start.9 = (bf16[1,256,2304]{2,1,0:T(8,128)(2,1)S(1)}, bf16[1,256,2304]{2,1,0:T(8,128)(2,1)}, u32[]{:S(2)}) copy-start(bf16[1,256,2304]{2,1,0:T(8,128)(2,1)} %param.14) | copy-start | bytes 3538948
  7.2 199.6 %all-gather.12.cloned.1.call-start = ((), (), s32[]{:S(2)}) async-start(), calls=%async_computation.3 | async-start | bytes 4423680 | tf_op jit(solution)/shard_map/all_gather | solution.py:91
  7.2 89.3 %collective-permute-start = (bf16[3,576,2304]{2,1,0:T(8,128)(2,1)}, bf16[3,576,2304]{2,1,0:T(8,128)(2,1)}, u32[]{:S(2)}, u32[]{:S(2)}) collective-permute-start(bf16[3,576,2304]{2,1,0:T(8,128)(2,1)} %param.20), channel_id=1, source_target_pairs={{0,1},{1,2},{2,3},{3,0},{4,5},{5,6},{6,7},{7,4},{8,9},{9,10},{10,1... | collective-permute-start | bytes 23887880 | tf_op jit(solution)/shard_map/ppermute | solution.py:104
  96.6 107.6 %collective-permute-start.1 = (bf16[3,576,2304]{2,1,0:T(8,128)(2,1)}, bf16[3,576,2304]{2,1,0:T(8,128)(2,1)}, u32[]{:S(2)}, u32[]{:S(2)}) collective-permute-start(bf16[3,576,2304]{2,1,0:T(8,128)(2,1)} %collective-permute-done), channel_id=1, source_target_pairs={{0,1},{1,2},{2,3},{3,0},{4,5},{5,6},{6,7},{7,4},{8,9},{9,10},{10,1... | collective-permute-start | bytes 23887880 | tf_op jit(solution)/shard_map/ppermute | solution.py:104
  98.7 144.3 %all-gather.14.cloned.1.call-start = ((), (), s32[]{:S(2)}) async-start(), calls=%async_computation.4 | async-start | bytes 3686400 | tf_op jit(solution)/shard_map/all_gather | solution.py:92
  204.1 104.4 %collective-permute-start.2 = (bf16[3,576,2304]{2,1,0:T(8,128)(2,1)}, bf16[3,576,2304]{2,1,0:T(8,128)(2,1)}, u32[]{:S(2)}, u32[]{:S(2)}) collective-permute-start(bf16[3,576,2304]{2,1,0:T(8,128)(2,1)} %collective-permute-done.1), channel_id=1, source_target_pairs={{0,1},{1,2},{2,3},{3,0},{4,5},{5,6},{6,7},{7,4},{8,9},{9,10},{10,1... | collective-permute-start | bytes 23887880 | tf_op jit(solution)/shard_map/ppermute | solution.py:104
  205.1 227.6 %all-gather.16.cloned.1.call-start = ((), (), s32[]{:S(2)}) async-start(), calls=%async_computation.5 | async-start | bytes 5898240 | tf_op jit(solution)/shard_map/all_gather | solution.py:127
  205.8 182.3 %copy-start.51 = (f32[2304]{0:T(1024)}, f32[2304]{0:T(1024)S(1)}, u32[]{:S(2)}) copy-start(f32[2304]{0:T(1024)S(1)} %convert_element_type.235) | copy-start | bytes 27652
  206.8 181.4 %copy-start.64 = (f32[256]{0:T(256)}, f32[256]{0:T(256)S(1)}, u32[]{:S(2)}) copy-start(f32[256]{0:T(256)S(1)} %fusion.126) | copy-start | bytes 3076
  208.2 39.7 %copy-start.57 = (bf16[3,16,256]{2,1,0:T(8,128)(2,1)}, bf16[3,16,256]{2,1,0:T(8,128)(2,1)S(1)}, u32[]{:S(2)}) copy-start(bf16[3,16,256]{2,1,0:T(8,128)(2,1)S(1)} %fusion.81) | copy-start | bytes 73732
  367.4 94.0 %all-gather.18.cloned.1.call-start = ((), (), s32[]{:S(2)}) async-start(), calls=%async_computation.6 | async-start | bytes 5898240 | tf_op jit(solution)/shard_map/all_gather | solution.py:126
  421.4 112.4 %all-gather.20.cloned.1.call-start = ((), (), s32[]{:S(2)}) async-start(), calls=%async_computation.7 | async-start | bytes 13271040 | tf_op jit(solution)/shard_map/all_gather | solution.py:145
  422.0 140.7 %all-gather.24.cloned.1.call-start = ((), (), s32[]{:S(2)}) async-start(), calls=%async_computation.9 | async-start | bytes 3686400 | tf_op jit(solution)/shard_map/all_gather | solution.py:94
  422.6 304.1 %all-gather.26.cloned.1.call-start = ((), (), s32[]{:S(2)}) async-start(), calls=%async_computation.10 | async-start | bytes 33177600 | tf_op jit(solution)/shard_map/all_gather | solution.py:176
  423.3 324.1 %all-gather.30.cloned.1.call-start = ((), (), s32[]{:S(2)}) async-start(), calls=%async_computation.15 | async-start | bytes 1843200 | tf_op jit(solution)/shard_map/all_gather | solution.py:93
  424.1 638.6 %all-gather.22.cloned.1.call-start = ((), (), s32[]{:S(2)}) async-start(), calls=%async_computation.8 | async-start | bytes 66355200 | tf_op jit(solution)/shard_map/all_gather | solution.py:164
  424.8 855.0 %reduce-scatter.13.cloned.1.call-start = ((), (), s32[]{:S(2)}) async-start(), calls=%async_computation.11 | async-start | bytes 5898240 | tf_op jit(solution)/shard_map/reduce_scatter | solution.py:272
  430.0 74.9 %copy-start.17 = (pred[256,1024]{1,0:T(8,128)(4,1)}, pred[256,1024]{1,0:T(8,128)(4,1)S(1)}, u32[]{:S(2)}) copy-start(pred[256,1024]{1,0:T(8,128)(4,1)S(1)} %fusion.91) | copy-start | bytes 786436
  432.7 35.3 %copy-start.7 = (bf16[256,2304]{0,1:T(8,128)(2,1)}, bf16[256,2304]{0,1:T(8,128)(2,1)S(1)}, u32[]{:S(2)}) copy-start(bf16[256,2304]{0,1:T(8,128)(2,1)S(1)} %copy.56) | copy-start | bytes 3538948
  487.3 17.6 copy-start.5
  541.9 599.0 %copy-start.1 = (f32[256,2304]{1,0:T(8,128)}, f32[256,2304]{1,0:T(8,128)S(1)}, u32[]{:S(2)}) copy-start(f32[256,2304]{1,0:T(8,128)S(1)} %get-tuple-element.42) | copy-start | bytes 7077892
  542.9 519.7 %copy-start.13 = (bf16[256,2304,1]{1,0,2:T(8,128)(2,1)}, bf16[256,2304,1]{1,0,2:T(8,128)(2,1)S(1)}, u32[]{:S(2)}) copy-start(bf16[256,2304,1]{1,0,2:T(8,128)(2,1)S(1)} %fusion.66) | copy-start | bytes 3538948
  1062.7 26.4 %copy-start.6 = (bf16[256,5760]{1,0:T(8,128)(2,1)S(1)}, bf16[256,5760]{1,0:T(8,128)(2,1)}, u32[]{:S(2)}) copy-start(bf16[256,5760]{1,0:T(8,128)(2,1)} %fusion.10) | copy-start | bytes 8847364
  1110.8 23.9 %copy-start.24 = (bf16[1,256,5760]{2,1,0:T(8,128)(2,1)S(1)}, bf16[1,256,5760]{2,1,0:T(8,128)(2,1)}, u32[]{:S(2)}) copy-start(bf16[1,256,5760]{2,1,0:T(8,128)(2,1)} %get-tuple-element.17) | copy-start | bytes 8847364
  1178.4 31.2 %copy-start.8 = (bf16[256,2304]{0,1:T(8,128)(2,1)S(1)}, bf16[256,2304]{0,1:T(8,128)(2,1)}, u32[]{:S(2)}) copy-start(bf16[256,2304]{0,1:T(8,128)(2,1)} %copy-done.7) | copy-start | bytes 3538948
  1221.6 98.6 %reduce-scatter.15.cloned.1.call-start = ((), (), s32[]{:S(2)}) async-start(), calls=%async_computation.12 | async-start | bytes 5898240 | tf_op jit(solution)/shard_map/reduce_scatter | solution.py:275
  1249.3 252.9 %all-reduce.14.cloned.1.call-start = ((), (), s32[]{:S(2)}) async-start(), calls=%async_computation.17 | async-start | bytes 18874368
  1331.5 201.6 %reduce-scatter.17.cloned.1.call-start = ((), (), s32[]{:S(2)}) async-start(), calls=%async_computation.14 | async-start | bytes 1843200 | tf_op jit(solution)/shard_map/reduce_scatter | solution.py:325
  1335.2 391.3 %all-gather.28.cloned.1.call-start = ((), (), s32[]{:S(2)}) async-start(), calls=%async_computation.13 | async-start | bytes 39813120 | tf_op jit(solution)/shard_map/all_gather | solution.py:299
  1335.8 515.1 %all-reduce.12.cloned.1.call-start = ((), (), s32[]{:S(2)}) async-start(), calls=%async_computation.16 | async-start | bytes 5455872 | tf_op jit(solution)/shard_map/psum | solution.py:333
  (61 other events, 310.5 us)
Sparse Core Ops, SparseCore 0:
  98.8 42.6 all-gather.11
  205.2 37.7 all-gather.13
  367.5 39.5 all-gather.15
  421.5 39.8 all-gather.17
  462.8 70.9 all-gather.19
  535.2 27.4 all-gather.23
  564.2 162.4 all-gather.25
  728.2 19.0 all-gather.29
  749.0 313.6 all-gather.21
  1221.7 47.8 reduce-scatter.12
  1272.2 47.8 reduce-scatter.14
  1331.6 170.5 all-reduce.13
  1505.3 27.6 reduce-scatter.16
  1534.5 191.9 all-gather.27
  1731.4 119.4 all-reduce.11
